TPU v7x, 512 devices: a whole 4x4x16 slice. The times are simulated.
512 devices in a mesh: expert: 64 (over y, z), tensor: 8 (over x, core).
Axes of the slice: x: 4, y: 4, z: 16, core: 2. Of those that a mesh axis runs over, the one named last changes fastest.
Arguments:
- tokens: bfloat16 [65536, 1024], P(('expert', 'tensor')), may hold values from -6 to 6
- out_grad: bfloat16 [65536, 1024], P(('expert', 'tensor')), may hold values from -6 to 6
- expert_ids: int32 [65536, 2], P(('expert', 'tensor')), may hold values from 0 to 63, all different within a row; in each aligned block of 128 rows (0 to 127, 128 to 255, ...) at most 5 rows name the same one
- gate_levels: int32 [65536, 2], P(('expert', 'tensor')), may hold values from 1 to 255
- gate_weight: bfloat16 [64, 1024, 2048], P('expert', None, 'tensor'), may hold values from -0.1875 to 0.1875
- up_weight: bfloat16 [64, 1024, 2048], P('expert', None, 'tensor'), may hold values from -0.1875 to 0.1875
- down_weight: bfloat16 [64, 1024, 2048], P('expert', None, 'tensor'), may hold values from -0.125 to 0.125
Outputs:
- token_grad: bfloat16 [65536, 1024], P(('expert', 'tensor'))
Inputs may be any that keep to these rules, and one draw needn't show every extreme that they name: `expert_ids`: A token's 2 experts differ. Among the 128 tokens of one device no expert is named more than 5 times, a bound that some block reaches.
All inputs are finite; a program needn't handle non-finite values.
Results may differ from a plain program's by a relative error of at most 0.01.
Values may be sent and summed in bfloat16 or wider, within the bound.
No kernel may reach another device: no remote copies, remote signals or barrier semaphores. Data moves between devices by JAX's collectives and lax.ppermute only.
A program may use at most 64 MiB of HBM per device.

v0:
```python
import jax
import jax.numpy as jnp
from jax import lax
from jax.sharding import PartitionSpec as P

level_scale = 1.0 / 256.0


def expert_grad(rows_in, grads_in, gate_cols, up_cols, down_cols):
    gate_pre = jnp.dot(rows_in, gate_cols, preferred_element_type=jnp.float32)
    up_pre = jnp.dot(rows_in, up_cols, preferred_element_type=jnp.float32)
    hidden_grad = jnp.dot(grads_in, down_cols, preferred_element_type=jnp.float32)
    sigmoid_val = jax.nn.sigmoid(gate_pre)
    up_grad = (hidden_grad * gate_pre * sigmoid_val).astype(jnp.bfloat16)
    gate_grad = (
        hidden_grad * up_pre * sigmoid_val * (1.0 + gate_pre * (1.0 - sigmoid_val))
    ).astype(jnp.bfloat16)
    joined_grad = jnp.concatenate([gate_grad, up_grad], axis=1)
    joined_cols = jnp.concatenate([gate_cols, up_cols], axis=1)
    back_dims = (((1,), (1,)), ((), ()))
    result = lax.dot_general(
        joined_grad, joined_cols, back_dims, preferred_element_type=jnp.float32
    )
    return result.astype(jnp.bfloat16)


def on_device(tokens, out_grad, expert_ids, gate_levels, gate_weight, up_weight, down_weight):
    tok_count, width = tokens.shape
    top_count = expert_ids.shape[1]
    experts = lax.axis_size("expert")
    capacity = max(2, 5 * tok_count * top_count // (4 * experts))
    slots = experts * capacity
    flat_ids = expert_ids.reshape(-1)
    lane_ids = jnp.arange(experts, dtype=jnp.int32)
    onehot = (flat_ids[:, None] == lane_ids[None, :]).astype(jnp.int32)
    slot_rank = jnp.sum(jnp.cumsum(onehot, axis=0) * onehot, axis=1) - 1
    slot_ids = flat_ids * capacity + slot_rank
    assign = (slot_ids[:, None] == jnp.arange(slots, dtype=jnp.int32)[None, :]).astype(jnp.float32)
    assign = assign.reshape(tok_count, top_count, slots)
    dispatch = jnp.sum(assign, axis=1).astype(jnp.bfloat16)
    route_scale = gate_levels.astype(jnp.float32) * level_scale
    combiner = jnp.sum(assign * route_scale[:, :, None], axis=1)
    send_dims = (((0,), (0,)), ((), ()))
    send_rows = lax.dot_general(
        dispatch, tokens, send_dims, preferred_element_type=jnp.float32
    ).astype(jnp.bfloat16)
    send_grads = lax.dot_general(
        dispatch, out_grad, send_dims, preferred_element_type=jnp.float32
    ).astype(jnp.bfloat16)
    packed = jnp.stack([send_rows, send_grads])
    received = lax.all_to_all(packed, "expert", split_axis=1, concat_axis=1, tiled=True)
    gate_cols = gate_weight[0]
    up_cols = up_weight[0]
    down_cols = down_weight[0]
    part_rows = lax.all_gather(received, "tensor", axis=1, tiled=True)
    partials = expert_grad(part_rows[0], part_rows[1], gate_cols, up_cols, down_cols)
    partials = partials.reshape(-1, slots, width)
    returned = lax.all_to_all(
        lax.all_to_all(partials, "expert", split_axis=1, concat_axis=1, tiled=True),
        "tensor",
        split_axis=0,
        concat_axis=0,
        tiled=True,
    )
    contrib = jnp.sum(returned.astype(jnp.float32), axis=0)
    token_grad = jnp.dot(
        combiner, contrib, precision=lax.Precision.HIGHEST, preferred_element_type=jnp.float32
    )
    return token_grad.astype(jnp.bfloat16)


def solution(mesh):
    return jax.shard_map(
        on_device,
        mesh=mesh,
        in_specs=(
            P(("expert", "tensor"), None),
            P(("expert", "tensor"), None),
            P(("expert", "tensor"), None),
            P(("expert", "tensor"), None),
            P("expert", None, "tensor"),
            P("expert", None, "tensor"),
            P("expert", None, "tensor"),
        ),
        out_specs=P(("expert", "tensor"), None),
        check_vma=False,
    )
```

profile of v0, /device:TPU:1, one launch (start us, length us, event | category | flops | bytes accessed | tf_op | source)
XLA Modules:
  0.0 501.7 jit_solution(4049381263710705938)
XLA Ops:
  6.5 0.0 copy-start
  6.5 0.0 all-gather.2.cloned.1.call-start
  6.5 0.8 copy.53
  7.4 0.1 eq.39
  7.5 0.1 eq.43
  7.7 0.6 reduce-window.6
  8.3 0.2 slice_reduce_fusion
  8.5 0.1 fusion.17
  8.6 0.1 sub.10
  8.8 0.1 copy.56
  8.8 0.7 multiply_add_fusion
  9.6 0.7 convert_multiply_fusion
  10.2 0.1 convert_reduce_fusion.1
  10.3 1.3 fusion.11
  11.6 1.3 fusion.10
  12.9 0.1 pad_maximum_fusion
  13.0 1.3 copy.57
  14.3 79.5 %all_to_all.15 = bf16[2,320,1024]{2,0,1:T(2,128)(2,1)S(1)} all-to-all(bf16[2,320,1024]{2,0,1:T(2,128)(2,1)S(1)} %copy.57), channel_id=1, replica_groups=mesh['expert'=64,'tensor'=8] {'expert'}, dimensions={1} | all-to-all | bytes 2621440 | tf_op jit(solution)/shard_map/all_to_all | solution.py:51
  93.9 0.0 copy-start.2
  93.9 1.4 copy.58
  95.3 0.0 all-gather.2.cloned.1.call-update
  95.3 64.1 %all-gather.2.cloned.1.call-done = bf16[2,2560,1024]{2,1,0:T(8,128)(2,1)} async-done(((bf16[2,320,1024]{2,1,0:T(8,128)(2,1)}), bf16[2,2560,1024]{2,1,0:T(8,128)(2,1)}) %all-gather.2.cloned.1.call-update) | async-done | bytes 10485776 | tf_op jit(solution)/shard_map/all_gather | solution.py:55
  159.4 0.0 copy-done.2
  159.5 0.0 copy-start.1
  159.5 4.2 fusion.1
  163.7 0.0 copy-done
  163.7 1.3 copy-done.1
  165.0 0.0 copy-start.3
  165.0 2.2 multiply_convert_fusion
  167.2 0.0 copy-done.3
  167.2 2.6 fusion.6
  169.7 3.2 convolution_convert_fusion
  173.0 2.9 copy.59
  175.9 245.5 %all_to_all.16 = bf16[8,320,1024]{2,0,1:T(8,128)(2,1)S(1)} all-to-all(bf16[8,320,1024]{2,0,1:T(8,128)(2,1)S(1)} %copy.59), channel_id=1, replica_groups=mesh['expert'=64,'tensor'=8] {'expert'}, dimensions={1} | all-to-all | bytes 10485760 | tf_op jit(solution)/shard_map/all_to_all | solution.py:59
  421.3 2.9 copy.60
  424.2 67.6 %all_to_all.17 = bf16[8,320,1024]{2,1,0:T(8,128)(2,1)S(1)} all-to-all(bf16[8,320,1024]{2,1,0:T(8,128)(2,1)S(1)} %copy.60), channel_id=1, replica_groups=mesh['expert'=64,'tensor'=8] {'tensor'}, dimensions={0} | all-to-all | bytes 10485760 | tf_op jit(solution)/shard_map/all_to_all | solution.py:58
  491.9 1.2 convert_reduce_fusion
  493.0 1.8 convolution_convert_fusion.3
  (4 shorter events, 0.1 us)
Async XLA Ops:
  6.5 157.2 %copy-start = (bf16[1,1024,256]{2,1,0:T(8,128)(2,1)S(1)}, bf16[1,1024,256]{2,1,0:T(8,128)(2,1)}, u32[]{:S(2)}) copy-start(bf16[1,1024,256]{2,1,0:T(8,128)(2,1)} %param.13) | copy-start | bytes 1572868
  6.5 152.9 %all-gather.2.cloned.1.call-start = ((), (), s32[]{:S(2)}) async-start(), calls=%async_computation.3 | async-start | bytes 11796480 | tf_op jit(solution)/shard_map/all_gather | solution.py:55
  93.9 65.6 %copy-start.2 = (bf16[1,1024,256]{2,1,0:T(8,128)(2,1)S(1)}, bf16[1,1024,256]{2,1,0:T(8,128)(2,1)}, u32[]{:S(2)}) copy-start(bf16[1,1024,256]{2,1,0:T(8,128)(2,1)} %param.11) | copy-start | bytes 1572868
  159.5 5.5 %copy-start.1 = (bf16[2,2560,1024]{2,1,0:T(8,128)(2,1)S(1)}, bf16[2,2560,1024]{2,1,0:T(8,128)(2,1)}, u32[]{:S(2)}) copy-start(bf16[2,2560,1024]{2,1,0:T(8,128)(2,1)} %all-gather.2.cloned.1.call-done) | copy-start | bytes 31457284
  165.0 2.2 copy-start.3
Sparse Core Ops, SparseCore 0:
  95.4 63.9 all-gather.1
where the time goes:
time: 502 us
  blocking collectives  393 us (78%)
  waiting for transfers between devices  64.2 us (13%)
  matrix products  16.5 us (3%)
  between operations  13.5 us (3%)
  local copies, waits for them, and re-layouts  11.4 us (2%)
    all_to_all x1, blocking collectives, on_device(): lax.all_to_all(partials, 'expert', split_axis=1, concat_axis=1, tiled=True)  245 us
    all_to_all x1, blocking collectives, on_device(): lax.all_to_all(packed, 'expert', split_axis=1, concat_axis=1, tiled=True)  79.5 us
    all_to_all x1, blocking collectives, on_device(): lax.all_to_all(lax.all_to_all(partials, 'expert', split_axis=1, concat_ax...  67.6 us
    all_gather x1, waiting for transfers between devices, on_device(): part_rows = lax.all_gather(received, 'tensor', axis=1, tiled=True)  64.1 us
  transfers between devices with their start and end apart: 1, of which 1 were waited for; matrix products, arithmetic and copies ran while one was open for 0% of the time, Pallas kernels for 0%

commit v1 on v0

--- a/solution.py
+++ b/solution.py
@@ -52,7 +52,10 @@
     gate_cols = gate_weight[0]
     up_cols = up_weight[0]
     down_cols = down_weight[0]
-    part_rows = lax.all_gather(received, "tensor", axis=1, tiled=True)
+    size = lax.axis_size("tensor")
+    blocks = jnp.stack([received for _ in range(size)])
+    blocks = lax.all_to_all(blocks, "tensor", split_axis=0, concat_axis=0)
+    part_rows = jnp.concatenate(blocks, axis=1)
     partials = expert_grad(part_rows[0], part_rows[1], gate_cols, up_cols, down_cols)
     partials = partials.reshape(-1, slots, width)
     returned = lax.all_to_all(

time: 502 us -> 556 us (1.11)
  blocking collectives: 393 us -> 512 us
  waiting for transfers between devices: 64.2 us -> 0 us
  between operations: 13.5 us -> 0.2 us
  local copies, waits for them, and re-layouts: 11.4 us -> 23.9 us
    all_to_all x0 -> x1, blocking collectives: none -> 128 us  [on_device(): blocks = lax.all_to_all(blocks, 'tensor', split_axis=0, concat_axis=0)]
    all_gather x1 -> x0, waiting for transfers between devices: 64.1 us -> none  [on_device(): part_rows = lax.all_gather(received, 'tensor', axis=1, tiled=True)]
    slice x1 -> x2, local copies, waits for them, and re-layouts: 0.18 us -> 9.84 us  [the longest x1 9.65 us: on_device(): part_rows[0]]
    all_to_all x1, blocking collectives: 245 us -> 236 us  [on_device(): lax.all_to_all(partials, 'expert', split_axis=1, concat_axis=1, tiled=True)]
  transfers between devices with their start and end apart: 1 -> 0, of which waited for: 1 -> 0; matrix products, arithmetic and copies ran while one was open for 0% -> 0% of each run, Pallas kernels for 0% -> 0%
where the time goes in v1:
time: 556 us
  blocking collectives  512 us (92%)
  local copies, waits for them, and re-layouts  23.9 us (4%)
  matrix products  16.3 us (3%)
    all_to_all x1, blocking collectives, on_device(): lax.all_to_all(partials, 'expert', split_axis=1, concat_axis=1, tiled=True)  236 us
    all_to_all x1, blocking collectives, on_device(): blocks = lax.all_to_all(blocks, 'tensor', split_axis=0, concat_axis=0)  128 us
    all_to_all x1, blocking collectives, on_device(): lax.all_to_all(packed, 'expert', split_axis=1, concat_axis=1, tiled=True)  79.6 us
    all_to_all x1, blocking collectives, on_device(): lax.all_to_all(lax.all_to_all(partials, 'expert', split_axis=1, concat_ax...  68.3 us

profile of v1, /device:TPU:1, one launch (start us, length us, event | category | flops | bytes accessed | tf_op | source)
XLA Modules:
  0.0 555.6 jit_solution(605586059623427668)
XLA Ops:
  0.0 0.0 copy-start
  0.0 0.8 copy.45
  0.8 0.1 eq.43
  1.0 0.1 eq.39
  1.1 0.7 convert_multiply_fusion
  1.8 0.6 reduce-window.6
  2.4 0.2 slice_reduce_fusion
  2.7 0.1 fusion.14
  2.8 0.1 sub.10
  2.9 0.1 copy.48
  3.0 0.7 multiply_add_fusion
  3.7 0.1 convert_reduce_fusion.1
  3.8 1.3 fusion.7
  5.0 1.3 fusion.6
  6.3 0.1 pad_maximum_fusion
  6.5 1.3 copy.49
  7.8 79.6 %all_to_all.20 = bf16[2,320,1024]{2,0,1:T(2,128)(2,1)S(1)} all-to-all(bf16[2,320,1024]{2,0,1:T(2,128)(2,1)S(1)} %copy.49), channel_id=1, replica_groups=mesh['expert'=64,'tensor'=8] {'expert'}, dimensions={1} | all-to-all | bytes 2621440 | tf_op jit(solution)/shard_map/all_to_all | solution.py:51
  87.4 0.3 copy.50
  87.7 5.2 stack.11
  93.0 127.8 %all_to_all.21 = bf16[8,2,320,1024]{3,2,1,0:T(8,128)(2,1)} all-to-all(bf16[8,2,320,1024]{3,2,1,0:T(8,128)(2,1)} %stack.11), channel_id=1, replica_groups=mesh['expert'=64,'tensor'=8] {'tensor'}, dimensions={0} | all-to-all | bytes 20971520 | tf_op jit(solution)/shard_map/all_to_all | solution.py:57
  220.7 0.0 copy-start.3
  220.8 9.7 %fusion.22 = (bf16[1,8,320,1024]{3,2,0,1:T(8,128)(2,1)}, bf16[1,8,320,1024]{3,2,0,1:T(8,128)(2,1)}) fusion(bf16[2,8,320,1024]{3,2,0,1:T(8,128)(2,1)} %bitcast.43), kind=kLoop, calls=%fused_computation.42 | loop fusion | bytes 20971520 | tf_op jit(solution)/shard_map/slice | solution.py:59
  230.4 0.0 copy-done.3
  230.4 0.0 copy-start.2
  230.4 0.0 slice-start
  230.4 4.2 fusion.19
  234.7 0.0 copy-done
  234.7 0.0 copy-done.2
  234.7 0.0 slice-start.1
  234.7 0.0 copy-start.4
  234.7 2.1 multiply_convert_fusion
  236.8 0.0 slice-done
  236.8 0.0 slice-done.1
  236.8 0.0 copy-done.4
  236.8 2.5 fusion.2
  239.3 3.2 convolution_convert_fusion
  242.5 2.9 copy.51
  245.4 236.1 %all_to_all.22 = bf16[8,320,1024]{2,0,1:T(8,128)(2,1)S(1)} all-to-all(bf16[8,320,1024]{2,0,1:T(8,128)(2,1)S(1)} %copy.51), channel_id=1, replica_groups=mesh['expert'=64,'tensor'=8] {'expert'}, dimensions={1} | all-to-all | bytes 10485760 | tf_op jit(solution)/shard_map/all_to_all | solution.py:62
  481.5 2.9 copy.52
  484.4 0.0 copy-start.1
  484.4 68.3 %all_to_all.23 = bf16[8,320,1024]{2,1,0:T(8,128)(2,1)S(1)} all-to-all(bf16[8,320,1024]{2,1,0:T(8,128)(2,1)S(1)} %copy.52), channel_id=1, replica_groups=mesh['expert'=64,'tensor'=8] {'tensor'}, dimensions={0} | all-to-all | bytes 10485760 | tf_op jit(solution)/shard_map/all_to_all | solution.py:61
  552.7 1.2 convert_reduce_fusion
  553.9 1.8 convolution_convert_fusion.3
  555.6 0.0 copy-done.1
  (5 shorter events, 0.1 us)
Async XLA Ops:
  0.0 234.7 %copy-start = (bf16[1,1024,256]{2,1,0:T(8,128)(2,1)S(1)}, bf16[1,1024,256]{2,1,0:T(8,128)(2,1)}, u32[]{:S(2)}) copy-start(bf16[1,1024,256]{2,1,0:T(8,128)(2,1)} %param.13) | copy-start | bytes 1572868
  220.7 9.7 %copy-start.3 = (bf16[1,1024,256]{2,1,0:T(8,128)(2,1)S(1)}, bf16[1,1024,256]{2,1,0:T(8,128)(2,1)}, u32[]{:S(2)}) copy-start(bf16[1,1024,256]{2,1,0:T(8,128)(2,1)} %param.11) | copy-start | bytes 1572868
  230.4 4.3 copy-start.2
  230.4 6.4 %slice-start = ((s8[5242880]{0:T(1024)(128)(4,1)}), s8[4194304]{0:T(1024)(128)(4,1)S(1)}, s32[]{:S(2)}) async-start(s8[5242880]{0:T(1024)(128)(4,1)} %bitcast.45), calls=%async_computation.4 | async-start | bytes 8388608
  234.7 2.1 slice-start.1
  234.7 2.1 copy-start.4
  484.4 71.2 %copy-start.1 = (bf16[1,1024,256]{2,1,0:T(8,128)(2,1)S(1)}, bf16[1,1024,256]{2,1,0:T(8,128)(2,1)}, u32[]{:S(2)}) copy-start(bf16[1,1024,256]{2,1,0:T(8,128)(2,1)} %param.13) | copy-start | bytes 1572868
